TPU v7x, 32 devices: a whole 2x2x4 slice. The times are simulated.
32 devices in a mesh: fsdp: 2 (over core), ctx: 4 (over y, x), tp: 4 (over z).
Axes of the slice: x: 2, y: 2, z: 4, core: 2. Of those that a mesh axis runs over, the one named last changes fastest.
Arguments:
- x_prompt: bfloat16 [2, 1024, 1024], P('fsdp', 'ctx'), may hold values from -6 to 6
- x_cont: bfloat16 [2, 12, 256, 1024], P('fsdp', 'ctx'), may hold values from -6 to 6
- cont_start: int32 [2, 12], P('fsdp', 'ctx'), may hold values from 512 to 1024
- w_qkv: bfloat16 [1024, 3, 1024], P(('fsdp', 'ctx'), None, 'tp'), may hold values from -0.1875 to 0.1875
- qkv_bias: bfloat16 [3, 1024], P(None, 'tp'), may hold values from -3 to 3
- w_dense: bfloat16 [1024, 1024], P('tp', ('fsdp', 'ctx')), may hold values from -0.75 to 0.75
- dense_bias: bfloat16 [1024], P(('fsdp', 'ctx')), may hold values from -3 to 3
- w_fc1: bfloat16 [1024, 4096], P(('fsdp', 'ctx'), 'tp'), may hold values from -0.1875 to 0.1875
- fc1_bias: bfloat16 [4096], P('tp'), may hold values from -3 to 3
- w_fc2: bfloat16 [4096, 1024], P('tp', ('fsdp', 'ctx')), may hold values from -0.09375 to 0.09375
- fc2_bias: bfloat16 [1024], P(('fsdp', 'ctx')), may hold values from -3 to 3
- ln1_gain: bfloat16 [1024], P(('fsdp', 'ctx')), may hold values from 0.099609375 to 1.8984375
- ln1_bias: bfloat16 [1024], P(('fsdp', 'ctx')), may hold values from -2 to 2
- ln2_gain: bfloat16 [1024], P(('fsdp', 'ctx')), may hold values from 0.099609375 to 1.8984375
- ln2_bias: bfloat16 [1024], P(('fsdp', 'ctx')), may hold values from -2 to 2
- dy_prompt: bfloat16 [2, 1024, 1024], P('fsdp', 'ctx'), may hold values from -6 to 6
- dy_cont: bfloat16 [2, 12, 256, 1024], P('fsdp', 'ctx'), may hold values from -6 to 6
Outputs:
- y_prompt: float32 [2, 1024, 1024], P('fsdp', 'ctx')
- y_cont: float32 [2, 12, 256, 1024], P('fsdp', 'ctx')
- dx_prompt: float32 [2, 1024, 1024], P('fsdp', 'ctx')
- dx_cont: float32 [2, 12, 256, 1024], P('fsdp', 'ctx')
- d_w_qkv: float32 [1024, 3, 1024], P(('fsdp', 'ctx'), None, 'tp')
- d_qkv_bias: float32 [3, 1024], P(None, 'tp')
- d_w_dense: float32 [1024, 1024], P('tp', ('fsdp', 'ctx'))
- d_dense_bias: float32 [1024], P(('fsdp', 'ctx'))
- d_w_fc1: float32 [1024, 4096], P(('fsdp', 'ctx'), 'tp')
- d_fc1_bias: float32 [4096], P('tp')
- d_w_fc2: float32 [4096, 1024], P('tp', ('fsdp', 'ctx'))
- d_fc2_bias: float32 [1024], P(('fsdp', 'ctx'))
- d_ln1_gain: float32 [1024], P(('fsdp', 'ctx'))
- d_ln1_bias: float32 [1024], P(('fsdp', 'ctx'))
- d_ln2_gain: float32 [1024], P(('fsdp', 'ctx'))
- d_ln2_bias: float32 [1024], P(('fsdp', 'ctx'))
Inputs may be any that keep to these rules, and one draw needn't show every extreme that they name: `cont_start`: a continuation follows the prompt tokens before its first position.
All inputs are finite; a program needn't handle non-finite values.
Results may differ from a plain program's by a relative error of at most 0.012.
Values may be sent and summed in bfloat16 or wider, within the bound.
A program may use at most 192 MiB of HBM per device.

v0:
```python
import jax
import jax.numpy as jnp
from jax import lax
from jax.sharding import PartitionSpec as P

HD = 64
ROT = 16
EPS = 1e-05


def layer_norm(inputs, norm_gain, norm_shift):
    row_mean = jnp.mean(inputs, axis=-1, keepdims=True)
    centered = inputs - row_mean
    variance = jnp.mean(centered * centered, axis=-1, keepdims=True)
    return centered * lax.rsqrt(variance + EPS) * norm_gain + norm_shift


def norm_pair(inputs, gain_one, shift_one, gain_two, shift_two):
    return (layer_norm(inputs, gain_one, shift_one), layer_norm(inputs, gain_two, shift_two))


def exact_gelu(values):
    return jax.nn.gelu(values, approximate=False)


def rotary_tables(positions):
    freq_index = jnp.arange(ROT // 2).astype(jnp.float32)
    inverse = jnp.power(10000.0, -2.0 * freq_index / ROT)
    phase = positions.astype(jnp.float32)[..., None] * inverse
    cos_half = jnp.cos(phase)
    sin_half = jnp.sin(phase)
    return (
        jnp.concatenate([cos_half, cos_half], axis=-1),
        jnp.concatenate([sin_half, sin_half], axis=-1),
    )


def rotate(inputs, cos_t, sin_t):
    leading = inputs[..., :ROT]
    half_rot = ROT // 2
    turned = jnp.concatenate([-leading[..., half_rot:], leading[..., :half_rot]], axis=-1)
    return jnp.concatenate([leading * cos_t + turned * sin_t, inputs[..., ROT:]], axis=-1)


def masked_scores(
    queries, all_keys, key_limit, query_slot, query_offs, prompt_len, key_slot, key_offs
):
    raw_scores = jnp.einsum("qhd,khd->hqk", queries, all_keys, preferred_element_type=jnp.float32)
    key_index = jnp.arange(all_keys.shape[0], dtype=jnp.int32)
    near_keys = key_index[None, :] < key_limit[:, None]
    own_keys = (key_slot[None, :] == query_slot[:, None]) & (
        key_offs[None, :] <= query_offs[:, None]
    )
    allowed = jnp.where((key_index < prompt_len)[None, :], near_keys, own_keys)
    return jnp.where(allowed[None], raw_scores * 0.125, -1e30)


def on_device(
    x_prompt,
    x_cont,
    cont_start,
    w_qkv,
    qkv_bias,
    w_dense,
    dense_bias,
    w_fc1,
    fc1_bias,
    w_fc2,
    fc2_bias,
    ln1_gain,
    ln1_bias,
    ln2_gain,
    ln2_bias,
    dy_prompt,
    dy_cont,
):
    gathered = (
        lax.all_gather(w_qkv, ("fsdp", "ctx"), axis=0, tiled=True),
        lax.all_gather(w_dense, ("fsdp", "ctx"), axis=1, tiled=True),
        lax.all_gather(w_fc1, ("fsdp", "ctx"), axis=0, tiled=True),
        lax.all_gather(w_fc2, ("fsdp", "ctx"), axis=1, tiled=True),
        lax.all_gather(dense_bias, ("fsdp", "ctx"), axis=0, tiled=True),
        lax.all_gather(fc2_bias, ("fsdp", "ctx"), axis=0, tiled=True),
        lax.all_gather(ln1_gain, ("fsdp", "ctx"), axis=0, tiled=True),
        lax.all_gather(ln1_bias, ("fsdp", "ctx"), axis=0, tiled=True),
        lax.all_gather(ln2_gain, ("fsdp", "ctx"), axis=0, tiled=True),
        lax.all_gather(ln2_bias, ("fsdp", "ctx"), axis=0, tiled=True),
    )
    qkv_full, dense_full, up_full, down_full = (gathered[0], gathered[1], gathered[2], gathered[3])
    dense_shift = gathered[4].astype(jnp.float32)
    down_shift = gathered[5].astype(jnp.float32)
    gain_one = gathered[6].astype(jnp.float32)
    shift_one = gathered[7].astype(jnp.float32)
    gain_two = gathered[8].astype(jnp.float32)
    shift_two = gathered[9].astype(jnp.float32)
    p_rows = x_prompt.shape[1]
    cont_count = x_cont.shape[1]
    cont_len = x_cont.shape[2]
    model_width = x_prompt.shape[2]
    row_count = p_rows + cont_count * cont_len
    prompt_len = p_rows * lax.axis_size("ctx")
    local_cols = qkv_full.shape[2]
    head_count = local_cols // HD
    piece_index = lax.axis_index("ctx")
    inputs = jnp.concatenate(
        [x_prompt[0], x_cont[0].reshape(cont_count * cont_len, model_width)], axis=0
    ).astype(jnp.float32)
    offsets = jnp.arange(cont_len, dtype=jnp.int32)
    prompt_pos = piece_index * p_rows + jnp.arange(p_rows, dtype=jnp.int32)
    starts = cont_start[0]
    cont_pos = (starts[:, None] + offsets[None, :]).reshape(cont_count * cont_len)
    positions = jnp.concatenate([prompt_pos, cont_pos])
    key_limit = jnp.concatenate([prompt_pos + 1, jnp.repeat(starts, cont_len)])
    own_slot = jnp.repeat(jnp.arange(cont_count, dtype=jnp.int32), cont_len)
    own_offs = jnp.tile(offsets, cont_count)
    query_slot = jnp.concatenate([jnp.full((p_rows,), -1, jnp.int32), own_slot])
    query_offs = jnp.concatenate([jnp.zeros((p_rows,), jnp.int32), own_offs])
    key_slot = jnp.concatenate([jnp.full((prompt_len,), -1, jnp.int32), own_slot])
    key_offs = jnp.concatenate([jnp.zeros((prompt_len,), jnp.int32), own_offs])
    cos_t, sin_t = rotary_tables(positions)
    cos_t = cos_t[:, None, :]
    sin_t = sin_t[:, None, :]
    norm_one, norm_two = norm_pair(inputs, gain_one, shift_one, gain_two, shift_two)
    ln_one = norm_one.astype(jnp.bfloat16)
    ln_two = norm_two.astype(jnp.bfloat16)
    qkv_flat = qkv_full.reshape(model_width, 3 * local_cols)
    projected = jnp.dot(ln_one, qkv_flat, preferred_element_type=jnp.float32) + qkv_bias.reshape(
        3 * local_cols
    ).astype(jnp.float32)
    projected = projected.reshape(row_count, 3, head_count, HD)
    queries = rotate(projected[:, 0], cos_t, sin_t).astype(jnp.bfloat16)
    keys_own = rotate(projected[:, 1], cos_t, sin_t).astype(jnp.bfloat16)
    values_own = projected[:, 2].astype(jnp.bfloat16)
    prompt_keys, prompt_values = (
        lax.all_gather(keys_own[:p_rows].reshape(p_rows, local_cols), "ctx", axis=0, tiled=True),
        lax.all_gather(values_own[:p_rows].reshape(p_rows, local_cols), "ctx", axis=0, tiled=True),
    )
    all_keys = jnp.concatenate(
        [prompt_keys.reshape(prompt_len, head_count, HD), keys_own[p_rows:]], axis=0
    )
    all_values = jnp.concatenate(
        [prompt_values.reshape(prompt_len, head_count, HD), values_own[p_rows:]], axis=0
    )
    scores = masked_scores(
        queries, all_keys, key_limit, query_slot, query_offs, prompt_len, key_slot, key_offs
    )
    highest = jnp.max(scores, axis=-1, keepdims=True)
    log_total = highest + jnp.log(jnp.sum(jnp.exp(scores - highest), axis=-1, keepdims=True))
    probs_low = jnp.exp(scores - log_total).astype(jnp.bfloat16)
    attended = jnp.einsum("hqk,khd->qhd", probs_low, all_values, preferred_element_type=jnp.float32)
    attended_low = attended.reshape(row_count, local_cols).astype(jnp.bfloat16)
    attn_part = jnp.dot(attended_low, dense_full, preferred_element_type=jnp.float32)
    hidden = jnp.dot(ln_two, up_full, preferred_element_type=jnp.float32) + fc1_bias.astype(
        jnp.float32
    )
    active_low = exact_gelu(hidden).astype(jnp.bfloat16)
    mlp_part = jnp.dot(active_low, down_full, preferred_element_type=jnp.float32)
    attn_total = lax.psum(attn_part, "tp")
    mlp_total = lax.psum(mlp_part.astype(jnp.bfloat16), "tp").astype(jnp.float32)
    mixed = attn_total + mlp_total
    output = inputs + mixed + dense_shift + down_shift
    again = (
        lax.all_gather(w_qkv, ("fsdp", "ctx"), axis=0, tiled=True),
        lax.all_gather(w_dense, ("fsdp", "ctx"), axis=1, tiled=True),
        lax.all_gather(w_fc1, ("fsdp", "ctx"), axis=0, tiled=True),
        lax.all_gather(w_fc2, ("fsdp", "ctx"), axis=1, tiled=True),
    )
    qkv_flat = again[0].reshape(model_width, 3 * local_cols)
    dense_full, up_full, down_full = (again[1], again[2], again[3])
    grad_out = jnp.concatenate(
        [dy_prompt[0], dy_cont[0].reshape(cont_count * cont_len, model_width)], axis=0
    )
    grad_dense = jnp.dot(attended_low.T, grad_out, preferred_element_type=jnp.float32)
    grad_down = jnp.dot(active_low.T, grad_out, preferred_element_type=jnp.float32)
    grad_shift = jnp.sum(grad_out.astype(jnp.float32), axis=0)
    grad_attended = (
        jnp.dot(grad_out, dense_full.T, preferred_element_type=jnp.float32)
        .astype(jnp.bfloat16)
        .reshape(row_count, head_count, HD)
    )
    scores = masked_scores(
        queries, all_keys, key_limit, query_slot, query_offs, prompt_len, key_slot, key_offs
    )
    probs = jnp.exp(scores - log_total)
    probs_low = probs.astype(jnp.bfloat16)
    grad_probs = jnp.einsum(
        "qhd,khd->hqk", grad_attended, all_values, preferred_element_type=jnp.float32
    )
    inner = jnp.sum(probs * grad_probs, axis=-1, keepdims=True)
    grad_scores = (probs * (grad_probs - inner)).astype(jnp.bfloat16)
    grad_queries = (
        jnp.einsum("hqk,khd->qhd", grad_scores, all_keys, preferred_element_type=jnp.float32)
        * 0.125
    )
    grad_keys = (
        jnp.einsum("hqk,qhd->khd", grad_scores, queries, preferred_element_type=jnp.float32) * 0.125
    )
    grad_values = jnp.einsum(
        "hqk,qhd->khd", probs_low, grad_attended, preferred_element_type=jnp.float32
    )
    prompt_key_grads, prompt_value_grads = (
        lax.psum_scatter(
            grad_keys[:prompt_len].reshape(prompt_len, local_cols),
            "ctx",
            scatter_dimension=0,
            tiled=True,
        ),
        lax.psum_scatter(
            grad_values[:prompt_len].reshape(prompt_len, local_cols),
            "ctx",
            scatter_dimension=0,
            tiled=True,
        ),
    )
    grad_keys = jnp.concatenate(
        [prompt_key_grads.reshape(p_rows, head_count, HD), grad_keys[prompt_len:]], axis=0
    )
    grad_values = jnp.concatenate(
        [prompt_value_grads.reshape(p_rows, head_count, HD), grad_values[prompt_len:]], axis=0
    )
    grad_projected = jnp.stack(
        [rotate(grad_queries, cos_t, -sin_t), rotate(grad_keys, cos_t, -sin_t), grad_values], axis=1
    )
    grad_proj_low = grad_projected.reshape(row_count, 3 * local_cols).astype(jnp.bfloat16)
    grad_qkv = jnp.dot(ln_one.T, grad_proj_low, preferred_element_type=jnp.float32).reshape(
        model_width, 3, local_cols
    )
    grad_qkv_bias = jnp.sum(grad_proj_low.astype(jnp.float32), axis=0).reshape(3, local_cols)
    grad_norm_one = jnp.dot(grad_proj_low, qkv_flat.T, preferred_element_type=jnp.float32)
    grad_active = jnp.dot(grad_out, down_full.T, preferred_element_type=jnp.float32)
    gelu_back = jax.vjp(exact_gelu, hidden)[1]
    grad_hidden_low = gelu_back(grad_active)[0].astype(jnp.bfloat16)
    grad_up = jnp.dot(ln_two.T, grad_hidden_low, preferred_element_type=jnp.float32)
    grad_up_bias = jnp.sum(grad_hidden_low.astype(jnp.float32), axis=0)
    grad_norm_two = jnp.dot(grad_hidden_low, up_full.T, preferred_element_type=jnp.float32)
    norm_back = jax.vjp(norm_pair, inputs, gain_one, shift_one, gain_two, shift_two)[1]
    full_one = lax.psum(grad_norm_one, "tp")
    full_two = lax.psum(grad_norm_two, "tp")
    grad_in, grad_gain_one, grad_shift_one, grad_gain_two, grad_shift_two = norm_back(
        (full_one, full_two)
    )
    grad_inputs = grad_in + grad_out.astype(jnp.float32)
    owned = (
        lax.psum_scatter(grad_qkv, ("fsdp", "ctx"), scatter_dimension=0, tiled=True),
        lax.psum_scatter(grad_dense, ("fsdp", "ctx"), scatter_dimension=1, tiled=True),
        lax.psum_scatter(grad_up, ("fsdp", "ctx"), scatter_dimension=0, tiled=True),
        lax.psum_scatter(grad_down, ("fsdp", "ctx"), scatter_dimension=1, tiled=True),
        lax.psum_scatter(grad_shift, ("fsdp", "ctx"), scatter_dimension=0, tiled=True),
        lax.psum_scatter(grad_gain_one, ("fsdp", "ctx"), scatter_dimension=0, tiled=True),
        lax.psum_scatter(grad_shift_one, ("fsdp", "ctx"), scatter_dimension=0, tiled=True),
        lax.psum_scatter(grad_gain_two, ("fsdp", "ctx"), scatter_dimension=0, tiled=True),
        lax.psum_scatter(grad_shift_two, ("fsdp", "ctx"), scatter_dimension=0, tiled=True),
    )
    bias_qkv_total, bias_up_total = lax.psum((grad_qkv_bias, grad_up_bias), ("fsdp", "ctx"))
    y_prompt = output[:p_rows][None]
    y_cont = output[p_rows:].reshape(1, cont_count, cont_len, model_width)
    dx_prompt = grad_inputs[:p_rows][None]
    dx_cont = grad_inputs[p_rows:].reshape(1, cont_count, cont_len, model_width)
    return (
        y_prompt,
        y_cont,
        dx_prompt,
        dx_cont,
        owned[0],
        bias_qkv_total,
        owned[1],
        owned[4],
        owned[2],
        bias_up_total,
        owned[3],
        owned[4],
        owned[5],
        owned[6],
        owned[7],
        owned[8],
    )


def solution(mesh):
    placed = (
        P("fsdp", "ctx", None),
        P("fsdp", "ctx", None, None),
        P("fsdp", "ctx"),
        P(("fsdp", "ctx"), None, "tp"),
        P(None, "tp"),
        P("tp", ("fsdp", "ctx")),
        P(("fsdp", "ctx")),
        P(("fsdp", "ctx"), "tp"),
        P("tp"),
        P("tp", ("fsdp", "ctx")),
        P(("fsdp", "ctx")),
        P(("fsdp", "ctx")),
        P(("fsdp", "ctx")),
        P(("fsdp", "ctx")),
        P(("fsdp", "ctx")),
        P("fsdp", "ctx", None),
        P("fsdp", "ctx", None, None),
    )
    return jax.shard_map(
        on_device,
        mesh=mesh,
        in_specs=placed,
        out_specs=(
            P("fsdp", "ctx", None),
            P("fsdp", "ctx", None, None),
            P("fsdp", "ctx", None),
            P("fsdp", "ctx", None, None),
            P(("fsdp", "ctx"), None, "tp"),
            P(None, "tp"),
            P("tp", ("fsdp", "ctx")),
            P(("fsdp", "ctx")),
            P(("fsdp", "ctx"), "tp"),
            P("tp"),
            P("tp", ("fsdp", "ctx")),
            P(("fsdp", "ctx")),
            P(("fsdp", "ctx")),
            P(("fsdp", "ctx")),
            P(("fsdp", "ctx")),
            P(("fsdp", "ctx")),
        ),
        check_vma=False,
    )
```

profile of v0, /device:TPU:0, one launch (start us, length us, event | category | flops | bytes accessed | tf_op | source)
XLA Modules:
  0.0 1037.2 jit_solution(66057958732764653)
XLA Ops:
  7.3 1.9 copy.36
  13.8 1.9 convert_reduce_fusion
  15.7 1.7 fusion.19
  18.0 14.7 %all-gather = bf16[8,1,128]{2,1,0:T(2,128)(2,1)S(1)} all-gather(bf16[1,1,128]{2,1,0:T(2,128)(2,1)S(1)} %bitcast.150), channel_id=1, replica_groups=mesh['fsdp'=2,'ctx'=4,'tp'=4] {'fsdp','ctx'}, dimensions={0}, use_global_device_ids=true | all-gather | bytes 2304 | tf_op jit(solution)/shard_map/all_gather | solution.py:84
  32.7 13.2 %all-gather.1 = bf16[8,1,128]{2,1,0:T(2,128)(2,1)S(1)} all-gather(bf16[1,1,128]{2,1,0:T(2,128)(2,1)S(1)} %bitcast.151), channel_id=1, replica_groups=mesh['fsdp'=2,'ctx'=4,'tp'=4] {'fsdp','ctx'}, dimensions={0}, use_global_device_ids=true | all-gather | bytes 2304 | tf_op jit(solution)/shard_map/all_gather | solution.py:85
  48.1 25.5 %all_gather.45 = bf16[256,1024]{1,0:T(8,128)(2,1)S(1)} all-gather(bf16[256,128]{1,0:T(8,128)(2,1)S(1)} %copy-done.22), channel_id=1, replica_groups=mesh['fsdp'=2,'ctx'=4,'tp'=4] {'fsdp','ctx'}, dimensions={1}, use_global_device_ids=true | all-gather | bytes 589824 | tf_op jit(solution)/shard_map/all_gather | solution.py:79
  73.6 12.2 %all-gather.2 = bf16[8,1,128]{2,1,0:T(2,128)(2,1)S(1)} all-gather(bf16[1,1,128]{2,1,0:T(2,128)(2,1)S(1)} %bitcast.153), channel_id=1, replica_groups=mesh['fsdp'=2,'ctx'=4,'tp'=4] {'fsdp','ctx'}, dimensions={0}, use_global_device_ids=true | all-gather | bytes 2304 | tf_op jit(solution)/shard_map/all_gather | solution.py:86
  85.8 13.8 %all-gather.3 = bf16[8,1,128]{2,1,0:T(2,128)(2,1)S(1)} all-gather(bf16[1,1,128]{2,1,0:T(2,128)(2,1)S(1)} %bitcast.154), channel_id=1, replica_groups=mesh['fsdp'=2,'ctx'=4,'tp'=4] {'fsdp','ctx'}, dimensions={0}, use_global_device_ids=true | all-gather | bytes 2304 | tf_op jit(solution)/shard_map/all_gather | solution.py:87
  100.9 2.6 convolution_convert_fusion.2
  103.5 3.9 fusion.2
  107.4 3.6 convolution_add_fusion
  111.9 12.9 %all_gather.44 = bf16[1024,256]{0,1:T(8,128)(2,1)S(1)} all-gather(bf16[256,256]{0,1:T(8,128)(2,1)S(1)} %bitcast.131), channel_id=1, replica_groups=mesh['fsdp'=2,'ctx'=4,'tp'=4] {'ctx'}, dimensions={0}, use_global_device_ids=true | all-gather | bytes 655360 | tf_op jit(solution)/shard_map/all_gather | solution.py:135
  124.8 12.9 %fusion = (f32[4,1024]{1,0:T(4,128)S(1)}, f32[4,1024,1792]{2,1,0:T(8,128)}) fusion(pred[1024,1792]{1,0:T(8,128)(4,1)S(1)} %fusion.2, bf16[1024,4,48]{0,2,1:T(8,128)(2,1)S(1)} %slice.216, bf16[1024,4,16]{0,2,1:T(8,128)(2,1)S(1)} %get-tuple-element.57, bf16[1024,4,64]{0,2,1:T(8,128)(2,1)S(1)} %bitcast.123, bf16[1024,4,48]{0,2,1:T(8,128)(2,1)S(1)} %slice.217, ...), kind=kOutput, calls=%fused_computation.5 | convolution fusion | flops 966717440 | bytes 32784384 | tf_op jit(solution)/shard_map/qhd,khd->hqk/dot_general | solution.py:48
  137.6 13.8 %exponential_reduce_fusion = f32[4,1024]{1,0:T(4,128)S(1)} fusion(f32[4,1024,1792]{2,1,0:T(8,128)} %get-tuple-element.66, f32[4,1024]{1,0:T(4,128)S(1)} %get-tuple-element.65, pred[1024,1792]{1,0:T(8,128)(4,1)S(1)} %fusion.2), kind=kLoop, calls=%fused_computation.3 | loop fusion | flops 29356032 | bytes 31227904 | tf_op jit(solution)/shard_map/reduce_sum | solution.py:148
  151.4 12.7 %all_gather.43 = bf16[1024,256]{0,1:T(8,128)(2,1)S(1)} all-gather(bf16[256,256]{0,1:T(8,128)(2,1)S(1)} %bitcast.132), channel_id=1, replica_groups=mesh['fsdp'=2,'ctx'=4,'tp'=4] {'ctx'}, dimensions={0}, use_global_device_ids=true | all-gather | bytes 655360 | tf_op jit(solution)/shard_map/all_gather | solution.py:136
  164.2 22.0 %multiply_reduce_fusion = (f32[4,1024]{1,0:T(4,128)S(1)}, f32[4,1024,1792]{2,1,0:T(8,128)}) fusion(f32[4,1024,1792]{2,1,0:T(8,128)} %get-tuple-element.66, f32[4,1024]{1,0:T(4,128)S(1)} %log_add_fusion, pred[1024,1792]{1,0:T(8,128)(4,1)S(1)} %fusion.2, bf16[1024,4,64]{0,2,1:T(8,128)(2,1)S(1)} %bitcast.129, bf16[768,4,64]{0,2,1:T(8,128)(2,1)S(1)} %slice_bitcast_fusion.4, ...), kind=kOutput, calls=%fused_computation.1 | convolution fusion | flops 978055168 | bytes 62029824 | tf_op jit(solution)/shard_map/qhd,khd->hqk/dot_general | solution.py:186
  186.2 24.6 %multiply_convert_fusion = bf16[4,1024,1792]{2,1,0:T(8,128)(2,1)} fusion(f32[4,1024,1792]{2,1,0:T(8,128)} %get-tuple-element.69, f32[4,1024,1792]{2,1,0:T(8,128)} %get-tuple-element.66, f32[4,1024]{1,0:T(4,128)S(1)} %get-tuple-element.68, f32[4,1024]{1,0:T(4,128)S(1)} %log_add_fusion, pred[1024,1792]{1,0:T(8,128)(4,1)S(1)} %fusion.2), kind=kLoop, calls=%fused_computation | loop fusion | flops 44040192 | bytes 75268096 | tf_op jit(solution)/shard_map/convert_element_type | solution.py:190
  210.8 7.8 fusion.30
  220.7 12.7 %convolution_bitcast_fusion = f32[1792,4,64]{0,2,1:T(8,128)S(1)} fusion(bf16[1024,4,64]{0,2,1:T(8,128)(2,1)S(1)} %bitcast.130, f32[4,1024,1792]{2,1,0:T(8,128)} %get-tuple-element.66, f32[4,1024]{1,0:T(4,128)S(1)} %log_add_fusion, pred[1024,1792]{1,0:T(8,128)(4,1)S(1)} %fusion.2), kind=kOutput, calls=%fused_computation.58 | convolution fusion | flops 968884224 | bytes 33570816 | tf_op jit(solution)/shard_map/hqk,qhd->khd/dot_general | solution.py:198
  235.3 9.7 fusion.35
  246.9 14.3 %convolution_convert_fusion.1 = bf16[4,64,1024]{2,1,0:T(8,128)(2,1)} fusion(bf16[768,4,64]{0,2,1:T(8,128)(2,1)} %copy-done.13, bf16[1024,4,64]{0,2,1:T(8,128)(2,1)} %bitcast.117, f32[4,1024,1792]{2,1,0:T(8,128)} %get-tuple-element.66, f32[4,1024]{1,0:T(4,128)S(1)} %log_add_fusion, pred[1024,1792]{1,0:T(8,128)(4,1)S(1)} %fusion.2), kind=kOutput, calls=%fused_computation.75 | convolution fusion | flops 970981376 | bytes 32653312 | tf_op jit(solution)/shard_map/hqk,khd->qhd/dot_general | solution.py:150
  261.2 4.0 fusion.78
  265.5 16.0 %multiply_convert_fusion.1 = (bf16[1024,1024]{1,0:T(8,128)(2,1)}, f32[1024,1024]{1,0:T(8,128)}, f32[1024,1024]{1,0:T(8,128)}) fusion(f32[1024]{0:T(1024)S(1)} %copy-done.26, bf16[1024,1024]{1,0:T(8,128)(2,1)} %all-gather.12.cloned.1.call-done, f32[1024]{0:T(1024)S(1)} %bitcast.148, f32[1024]{0:T(1024)S(1)} %bitcast.139, f32[1024]{0:T(1024)S(1)} %fusion.55, ...), kind=kOutput, calls=%fused_computation.41 | convolution fusion | flops 2226126848 | bytes 14700544 | tf_op jit(solution)/shard_map/dot_general | solution.py:153
  281.5 9.1 convert_reduce_fusion.2
  292.0 4.4 fusion.79
  298.3 1.8 fusion.38
  300.2 5.3 reduce-scatter.9.cloned.1.call-done
  306.7 1.3 convert_reduce_fusion.3
  309.2 3.8 fusion.80
  313.4 6.0 convolution_convert_fusion
  319.5 3.3 fusion.73
  322.8 5.3 fusion.31
  328.2 6.2 fusion.64
  334.5 6.4 fusion.72
  341.5 13.7 %all-gather.4 = bf16[8,1,128]{2,1,0:T(2,128)(2,1)S(1)} all-gather(bf16[1,1,128]{2,1,0:T(2,128)(2,1)S(1)} %bitcast.155), channel_id=1, replica_groups=mesh['fsdp'=2,'ctx'=4,'tp'=4] {'fsdp','ctx'}, dimensions={0}, use_global_device_ids=true | all-gather | bytes 2304 | tf_op jit(solution)/shard_map/all_gather | solution.py:82
  355.2 13.4 %all-gather.5 = bf16[8,1,128]{2,1,0:T(2,128)(2,1)S(1)} all-gather(bf16[1,1,128]{2,1,0:T(2,128)(2,1)S(1)} %bitcast.156), channel_id=1, replica_groups=mesh['fsdp'=2,'ctx'=4,'tp'=4] {'fsdp','ctx'}, dimensions={0}, use_global_device_ids=true | all-gather | bytes 2304 | tf_op jit(solution)/shard_map/all_gather | solution.py:83
  369.8 370.8 %all-reduce.16.cloned.1.call-done = (f32[1024,1024]{1,0:T(8,128)}, f32[1024,1024]{1,0:T(8,128)}, f32[1024,1024]{1,0:T(8,128)}) async-done(((f32[1024,1024]{1,0:T(8,128)}, f32[1024,1024]{1,0:T(8,128)}, f32[1024,1024]{1,0:T(8,128)}), (f32[1024,1024]{1,0:T(8,128)}, f32[1024,1024]{1,0:T(8,128)}, f32[1024,1024]{1,0:T(8,128)})) %all-reduce.16.cloned.1.call-update) | async-done | bytes 12582928 | tf_op jit(solution)/shard_map/psum | solution.py:158
  740.7 4.7 fusion.76
  745.4 83.7 %all-reduce.14.cloned.1.call-done = bf16[1024,1024]{1,0:T(8,128)(2,1)} async-done(((bf16[1024,1024]{1,0:T(8,128)(2,1)}), bf16[1024,1024]{1,0:T(8,128)(2,1)}) %all-reduce.14.cloned.1.call-update) | async-done | bytes 2097168 | tf_op jit(solution)/shard_map/psum | solution.py:159
  829.1 9.3 fusion.18
  838.4 5.4 convert_reduce_fusion.1
  843.8 26.6 %all-reduce.9 = (f32[3,256]{1,0:T(4,128)}, f32[1024]{0:T(1024)S(1)}, f32[1024]{0:T(1024)}, f32[1024]{0:T(1024)S(1)}, f32[1024]{0:T(1024)S(1)}, /*index=5*/f32[1024]{0:T(1024)S(1)}, f32[1024]{0:T(1024)S(1)}) all-reduce(f32[3,256]{1,0:T(4,128)S(1)} %reshape.336, ...), channel_id=1, replica_groups=mesh['fsdp'=2,'ctx'=4,'tp'=4] {'fsdp','ctx'}, use_global_device_ids=true, to_apply=%region_17.18 | all-reduce | flops 6912 | bytes 55296 | tf_op jit(solution)/shard_map/psum | solution.py:254
  872.8 4.0 slice.168
  876.8 1.9 slice.152
  878.7 2.3 slice_bitcast_fusion
  882.0 36.9 %reduce-scatter.11.cloned.1.call-done = f32[128,3,256]{2,0,1:T(8,128)} async-done(((f32[1024,3,256]{2,0,1:T(8,128)}), f32[128,3,256]{2,0,1:T(8,128)}) %reduce-scatter.11.cloned.1.call-update) | async-done | bytes 393232 | tf_op jit(solution)/shard_map/reduce_scatter | solution.py:244
  919.0 55.1 %reduce-scatter.15.cloned.1.call-done = f32[128,1024]{1,0:T(8,128)} async-done(((f32[1024,1024]{1,0:T(8,128)}), f32[128,1024]{1,0:T(8,128)}) %reduce-scatter.15.cloned.1.call-update) | async-done | bytes 524304 | tf_op jit(solution)/shard_map/reduce_scatter | solution.py:246
  974.1 55.6 %reduce-scatter.17.cloned.1.call-done = f32[1024,128]{1,0:T(8,128)} async-done(((f32[1024,1024]{1,0:T(8,128)}), f32[1024,128]{1,0:T(8,128)}) %reduce-scatter.17.cloned.1.call-update) | async-done | bytes 524304 | tf_op jit(solution)/shard_map/reduce_scatter | solution.py:247
  (176 shorter events, 27.1 us)
Async XLA Ops:
  7.2 8.5 copy-start
  7.2 10.8 %copy-start.32 = (bf16[128]{0:T(256)(128)(2,1)S(1)}, bf16[128]{0:T(256)(128)(2,1)}, u32[]{:S(2)}) copy-start(bf16[128]{0:T(256)(128)(2,1)} %param.28) | copy-start | bytes 772
  7.2 25.5 %copy-start.33 = (bf16[128]{0:T(256)(128)(2,1)S(1)}, bf16[128]{0:T(256)(128)(2,1)}, u32[]{:S(2)}) copy-start(bf16[128]{0:T(256)(128)(2,1)} %param.29) | copy-start | bytes 772
  7.2 39.3 %copy-start.30 = (bf16[3,256]{1,0:T(4,128)(2,1)S(1)}, bf16[3,256]{1,0:T(4,128)(2,1)}, u32[]{:S(2)}) copy-start(bf16[3,256]{1,0:T(4,128)(2,1)} %param.21) | copy-start | bytes 4612
  7.2 39.9 %copy-start.34 = (s32[1,3]{1,0:T(1,128)S(1)}, s32[1,3]{1,0:T(1,128)}, u32[]{:S(2)}) copy-start(s32[1,3]{1,0:T(1,128)} %param.19) | copy-start | bytes 40
  7.2 40.9 %copy-start.22 = (bf16[256,128]{1,0:T(8,128)(2,1)S(1)}, bf16[256,128]{1,0:T(8,128)(2,1)}, u32[]{:S(2)}) copy-start(bf16[256,128]{1,0:T(8,128)(2,1)} %param.22) | copy-start | bytes 196612
  7.2 66.3 %copy-start.35 = (bf16[128]{0:T(256)(128)(2,1)S(1)}, bf16[128]{0:T(256)(128)(2,1)}, u32[]{:S(2)}) copy-start(bf16[128]{0:T(256)(128)(2,1)} %param.30) | copy-start | bytes 772
  7.3 78.6 %copy-start.36 = (bf16[128]{0:T(256)(128)(2,1)S(1)}, bf16[128]{0:T(256)(128)(2,1)}, u32[]{:S(2)}) copy-start(bf16[128]{0:T(256)(128)(2,1)} %param.31) | copy-start | bytes 772
  7.3 93.0 %copy-start.31 = (bf16[1024]{0:T(1024)(128)(2,1)S(1)}, bf16[1024]{0:T(1024)(128)(2,1)}, u32[]{:S(2)}) copy-start(bf16[1024]{0:T(1024)(128)(2,1)} %param.25) | copy-start | bytes 6148
  7.3 93.6 %copy-start.6 = (bf16[1,3,256,1024]{3,2,1,0:T(8,128)(2,1)S(1)}, bf16[1,3,256,1024]{3,2,1,0:T(8,128)(2,1)}, u32[]{:S(2)}) copy-start(bf16[1,3,256,1024]{3,2,1,0:T(8,128)(2,1)} %param.33) | copy-start | bytes 4718596
  7.3 100.1 %all-gather.10.cloned.1.call-start = ((), (), s32[]{:S(2)}) async-start(), calls=%async_computation.6 | async-start | bytes 1769472 | tf_op jit(solution)/shard_map/all_gather | solution.py:78
  9.2 256.2 %all-gather.12.cloned.1.call-start = ((), (), s32[]{:S(2)}) async-start(), calls=%async_computation.7 | async-start | bytes 2359296 | tf_op jit(solution)/shard_map/all_gather | solution.py:80
  10.0 271.5 %all-gather.14.cloned.1.call-start = ((), (), s32[]{:S(2)}) async-start(), calls=%async_computation.8 | async-start | bytes 2359296 | tf_op jit(solution)/shard_map/all_gather | solution.py:81
  10.7 285.6 %reduce-scatter.7.cloned.1.call-start = ((), (), s32[]{:S(2)}) async-start(), calls=%async_computation.10 | async-start | bytes 1310720 | tf_op jit(solution)/shard_map/reduce_scatter | solution.py:202
  32.7 74.7 %copy-start.20 = (f32[8,1,128]{2,1,0:T(1,128)}, f32[8,1,128]{2,1,0:T(1,128)S(1)}, u32[]{:S(2)}) copy-start(f32[8,1,128]{2,1,0:T(1,128)S(1)} %convert_element_type.144) | copy-start | bytes 12292
  48.1 63.7 %copy-start.16 = (f32[1024,16]{0,1:T(8,128)}, f32[1024,16]{0,1:T(8,128)S(1)}, u32[]{:S(2)}) copy-start(f32[1024,16]{0,1:T(8,128)S(1)} %pad_maximum_fusion.9) | copy-start | bytes 196612
  73.6 29.9 %copy-start.11 = (bf16[256,1024]{1,0:T(8,128)(2,1)}, bf16[256,1024]{1,0:T(8,128)(2,1)S(1)}, u32[]{:S(2)}) copy-start(bf16[256,1024]{1,0:T(8,128)(2,1)S(1)} %all_gather.45) | copy-start | bytes 1572868
  111.7 52.4 %copy-start.13 = (bf16[768,4,64]{0,2,1:T(8,128)(2,1)}, bf16[768,4,64]{0,2,1:T(8,128)(2,1)S(1)}, u32[]{:S(2)}) copy-start(bf16[768,4,64]{0,2,1:T(8,128)(2,1)S(1)} %slice_bitcast_fusion.4) | copy-start | bytes 1179652
  137.6 26.6 %copy-start.18 = (bf16[1024,256]{0,1:T(8,128)(2,1)S(1)}, bf16[1024,256]{0,1:T(8,128)(2,1)}, u32[]{:S(2)}) copy-start(bf16[1024,256]{0,1:T(8,128)(2,1)} %convolution_convert_fusion.2) | copy-start | bytes 1572868
  164.2 22.0 %copy-start.9 = (bf16[1024,256]{0,1:T(8,128)(2,1)}, bf16[1024,256]{0,1:T(8,128)(2,1)S(1)}, u32[]{:S(2)}) copy-start(bf16[1024,256]{0,1:T(8,128)(2,1)S(1)} %all_gather.43) | copy-start | bytes 1572868
  246.8 58.7 %reduce-scatter.9.cloned.1.call-start = ((), (), s32[]{:S(2)}) async-start(), calls=%async_computation.11 | async-start | bytes 1310720 | tf_op jit(solution)/shard_map/reduce_scatter | solution.py:208
  261.2 4.2 copy-start.4
  261.2 4.2 copy-start.26
  261.2 4.3 copy-start.28
  265.2 475.5 %all-reduce.16.cloned.1.call-start = ((), (), s32[]{:S(2)}) async-start(), calls=%async_computation.16 | async-start | bytes 25165824 | tf_op jit(solution)/shard_map/psum | solution.py:158
  265.5 16.0 %copy-start.10 = (bf16[1,256,1024]{2,1,0:T(8,128)(2,1)S(1)}, bf16[1,256,1024]{2,1,0:T(8,128)(2,1)}, u32[]{:S(2)}) copy-start(bf16[1,256,1024]{2,1,0:T(8,128)(2,1)} %param.32) | copy-start | bytes 1572868
  281.5 10.4 %copy-start.39 = (bf16[1024,1024]{1,0:T(8,128)(2,1)S(1)}, bf16[1024,1024]{1,0:T(8,128)(2,1)}, u32[]{:S(2)}) copy-start(bf16[1024,1024]{1,0:T(8,128)(2,1)} %all-gather.12.cloned.1.call-done) | copy-start | bytes 6291460
  291.9 4.4 copy-start.5
  291.9 5.2 copy-start.17
  291.9 5.2 copy-start.19
  296.3 3.8 copy-start.14
  305.5 3.7 copy-start.40
  313.1 516.0 %all-reduce.14.cloned.1.call-start = ((), (), s32[]{:S(2)}) async-start(), calls=%async_computation.9 | async-start | bytes 4194304 | tf_op jit(solution)/shard_map/psum | solution.py:159
  313.3 6.1 copy-start.12
  319.4 562.6 %reduce-scatter.13.cloned.1.call-start = ((), (), s32[]{:S(2)}) async-start(), calls=%async_computation.13 | async-start | bytes 1179648 | tf_op jit(solution)/shard_map/reduce_scatter | solution.py:245
  322.7 596.2 %reduce-scatter.11.cloned.1.call-start = ((), (), s32[]{:S(2)}) async-start(), calls=%async_computation.12 | async-start | bytes 3538944 | tf_op jit(solution)/shard_map/reduce_scatter | solution.py:244
  322.8 5.4 copy-start.29
  328.1 646.0 %reduce-scatter.15.cloned.1.call-start = ((), (), s32[]{:S(2)}) async-start(), calls=%async_computation.14 | async-start | bytes 4718592 | tf_op jit(solution)/shard_map/reduce_scatter | solution.py:246
  334.4 695.3 %reduce-scatter.17.cloned.1.call-start = ((), (), s32[]{:S(2)}) async-start(), calls=%async_computation.15 | async-start | bytes 4718592 | tf_op jit(solution)/shard_map/reduce_scatter | solution.py:247
  340.8 14.3 %copy-start.38 = (bf16[128]{0:T(256)(128)(2,1)S(1)}, bf16[128]{0:T(256)(128)(2,1)}, u32[]{:S(2)}) copy-start(bf16[128]{0:T(256)(128)(2,1)} %param.27) | copy-start | bytes 772
  340.8 27.7 %copy-start.41 = (u32[32]{0:T(128)S(1)}, u32[32]{0:T(128)}, u32[]{:S(2)}) copy-start(u32[32]{0:T(128)} %constant.122) | copy-start | bytes 388
  740.7 4.7 copy-start.24
  829.1 9.3 copy-start.1
  829.1 9.3 copy-start.2
  829.1 9.3 copy-start.7
  838.4 5.4 copy-start.25
  870.4 6.4 copy-start.3
  870.5 159.3 %copy-start.42 = (f32[128]{0:T(128)}, f32[128]{0:T(128)S(1)}, u32[]{:S(2)}) copy-start(f32[128]{0:T(128)S(1)} %dynamic-slice.1) | copy-start | bytes 1540
  (7 other events, 11.7 us)
Sparse Core Ops, SparseCore 0:
  10.6 28.5 all-gather.9
  41.1 33.7 all-gather.11
  76.8 28.1 all-gather.13
  246.9 27.1 reduce-scatter.6
  277.7 27.7 reduce-scatter.8
  313.2 427.4 all-reduce.15
  743.6 85.4 all-reduce.13
  833.1 35.1 reduce-scatter.12
  872.7 46.2 reduce-scatter.10
  922.7 51.3 reduce-scatter.14
  978.4 51.2 reduce-scatter.16
where the time goes:
time: 1050 us; the launch traced here: 1040 us
  waiting for transfers between devices  609 us (58%)
  blocking collectives  159 us (15%)
  matrix products  150 us (14%)
  other arithmetic  76 us (7%)
  local copies, waits for them, and re-layouts  27.1 us (3%)
  between operations  15.5 us (1%)
    psum x1, waiting for transfers between devices, on_device(): attn_total = lax.psum(attn_part, 'tp')  371 us
    psum x1, waiting for transfers between devices, on_device(): lax.psum(mlp_part.astype(jnp.bfloat16), 'tp').astype(jnp.float32)  83.7 us
    reduce_scatter x1, waiting for transfers between devices, on_device(): lax.psum_scatter(grad_down, ('fsdp', 'ctx'), scatter_dimension=1, tiled=T...  55.6 us
    reduce_scatter x1, waiting for transfers between devices, on_device(): lax.psum_scatter(grad_up, ('fsdp', 'ctx'), scatter_dimension=0, tiled=True)  55.1 us
    reduce_scatter x1, waiting for transfers between devices, on_device(): lax.psum_scatter(grad_qkv, ('fsdp', 'ctx'), scatter_dimension=0, tiled=True)  36.9 us
    psum x1, blocking collectives, on_device(): lax.psum((grad_qkv_bias, grad_up_bias), ('fsdp', 'ctx'))  26.6 us
    all_gather x1, blocking collectives, on_device(): lax.all_gather(w_dense, ('fsdp', 'ctx'), axis=1, tiled=True)  25.5 us
    convert_element_type x1, other arithmetic, on_device(): grad_scores = (probs * (grad_probs - inner)).astype(jnp.bfloat16)  24.6 us
  transfers between devices with their start and end apart: 11, of which 6 were waited for; matrix products, arithmetic and copies ran while one was open for 23% of the time, Pallas kernels for 0%

commit v1 on v0

--- a/solution.py
+++ b/solution.py
@@ -6,6 +6,18 @@
 HD = 64
 ROT = 16
 EPS = 1e-05
+
+
+def doubled_up(value, axis, dim):
+    ways, here, step = (lax.axis_size(axis), lax.axis_index(axis), value.shape[dim])
+    line, have = (value, 1)
+    while have < ways:
+        line = jnp.concatenate(
+            [line, lax.ppermute(line, axis, [(d, (d - have) % ways) for d in range(ways)])],
+            axis=dim,
+        )
+        have = 2 * have
+    return jnp.roll(line, here * step, axis=dim)
 
 
 def layer_norm(inputs, norm_gain, norm_shift):
@@ -76,7 +88,7 @@
 ):
     gathered = (
         lax.all_gather(w_qkv, ("fsdp", "ctx"), axis=0, tiled=True),
-        lax.all_gather(w_dense, ("fsdp", "ctx"), axis=1, tiled=True),
+        doubled_up(w_dense, ("fsdp", "ctx"), 1),
         lax.all_gather(w_fc1, ("fsdp", "ctx"), axis=0, tiled=True),
         lax.all_gather(w_fc2, ("fsdp", "ctx"), axis=1, tiled=True),
         lax.all_gather(dense_bias, ("fsdp", "ctx"), axis=0, tiled=True),

time: 1050 us -> 1070 us (1.019)
  transfers between devices with their start and end apart: 11 -> 14, of which waited for: 6 -> 7; matrix products, arithmetic and copies ran while one was open for 23% -> 24% of each run, Pallas kernels for 0% -> 0%
where the time goes in v1:
time: 1070 us; the launch traced here: 1060 us
  waiting for transfers between devices  613 us (57%)
  blocking collectives  158 us (15%)
  matrix products  150 us (14%)
  other arithmetic  77 us (7%)
  local copies, waits for them, and re-layouts  36.6 us (3%)
  between operations  15.5 us (1%)
    psum x1, waiting for transfers between devices, on_device(): attn_total = lax.psum(attn_part, 'tp')  371 us
    psum x1, waiting for transfers between devices, on_device(): lax.psum(mlp_part.astype(jnp.bfloat16), 'tp').astype(jnp.float32)  83.7 us
    reduce_scatter x1, waiting for transfers between devices, on_device(): lax.psum_scatter(grad_down, ('fsdp', 'ctx'), scatter_dimension=1, tiled=T...  55.6 us
    reduce_scatter x1, waiting for transfers between devices, on_device(): lax.psum_scatter(grad_up, ('fsdp', 'ctx'), scatter_dimension=0, tiled=True)  55.1 us
    reduce_scatter x1, waiting for transfers between devices, on_device(): lax.psum_scatter(grad_qkv, ('fsdp', 'ctx'), scatter_dimension=0, tiled=True)  36.9 us
    psum x1, blocking collectives, on_device(): lax.psum((grad_qkv_bias, grad_up_bias), ('fsdp', 'ctx'))  26.6 us
    convert_element_type x1, other arithmetic, on_device(): grad_scores = (probs * (grad_probs - inner)).astype(jnp.bfloat16)  24.6 us
    all_gather x1, blocking collectives, on_device(): lax.all_gather(w_dense, ('fsdp', 'ctx'), axis=1, tiled=True)  23 us
  transfers between devices with their start and end apart: 14, of which 7 were waited for; matrix products, arithmetic and copies ran while one was open for 24% of the time, Pallas kernels for 0%

profile of v1, /device:TPU:0, one launch (start us, length us, event | category | flops | bytes accessed | tf_op | source)
XLA Modules:
  0.0 1056.9 jit_solution(5747467930660462979)
XLA Ops:
  7.3 1.9 copy.36
  10.0 3.4 collective-permute-start
  15.9 23.0 %all_gather.50 = bf16[256,1024]{1,0:T(8,128)(2,1)S(1)} all-gather(bf16[256,128]{1,0:T(8,128)(2,1)} %param.22), channel_id=1, replica_groups=mesh['fsdp'=2,'ctx'=4,'tp'=4] {'fsdp','ctx'}, dimensions={1}, use_global_device_ids=true | all-gather | bytes 589824 | tf_op jit(solution)/shard_map/all_gather | solution.py:176
  38.9 1.9 convert_reduce_fusion
  41.8 2.9 convolution_convert_fusion.2
  44.7 3.8 fusion.2
  48.6 2.2 collective-permute-start.1
  52.1 4.1 collective-permute-done.1
  58.3 13.7 %all-gather = bf16[8,1,128]{2,1,0:T(2,128)(2,1)S(1)} all-gather(bf16[1,1,128]{2,1,0:T(2,128)(2,1)} %bitcast.150), channel_id=1, replica_groups=mesh['fsdp'=2,'ctx'=4,'tp'=4] {'fsdp','ctx'}, dimensions={0}, use_global_device_ids=true | all-gather | bytes 2304 | tf_op jit(solution)/shard_map/all_gather | solution.py:96
  72.0 14.1 %all-gather.1 = bf16[8,1,128]{2,1,0:T(2,128)(2,1)S(1)} all-gather(bf16[1,1,128]{2,1,0:T(2,128)(2,1)} %bitcast.151), channel_id=1, replica_groups=mesh['fsdp'=2,'ctx'=4,'tp'=4] {'fsdp','ctx'}, dimensions={0}, use_global_device_ids=true | all-gather | bytes 2304 | tf_op jit(solution)/shard_map/all_gather | solution.py:97
  88.0 13.3 %all-gather.2 = bf16[8,1,128]{2,1,0:T(2,128)(2,1)S(1)} all-gather(bf16[1,1,128]{2,1,0:T(2,128)(2,1)} %bitcast.152), channel_id=1, replica_groups=mesh['fsdp'=2,'ctx'=4,'tp'=4] {'fsdp','ctx'}, dimensions={0}, use_global_device_ids=true | all-gather | bytes 2304 | tf_op jit(solution)/shard_map/all_gather | solution.py:98
  101.3 14.1 %all-gather.3 = bf16[8,1,128]{2,1,0:T(2,128)(2,1)S(1)} all-gather(bf16[1,1,128]{2,1,0:T(2,128)(2,1)} %bitcast.153), channel_id=1, replica_groups=mesh['fsdp'=2,'ctx'=4,'tp'=4] {'fsdp','ctx'}, dimensions={0}, use_global_device_ids=true | all-gather | bytes 2304 | tf_op jit(solution)/shard_map/all_gather | solution.py:99
  125.7 3.6 convolution_add_fusion
  130.5 13.0 %all_gather.43 = bf16[1024,256]{0,1:T(8,128)(2,1)S(1)} all-gather(bf16[256,256]{0,1:T(8,128)(2,1)S(1)} %bitcast.130), channel_id=1, replica_groups=mesh['fsdp'=2,'ctx'=4,'tp'=4] {'ctx'}, dimensions={0}, use_global_device_ids=true | all-gather | bytes 655360 | tf_op jit(solution)/shard_map/all_gather | solution.py:147
  143.5 12.8 %fusion = (f32[4,1024]{1,0:T(4,128)S(1)}, f32[4,1024,1792]{2,1,0:T(8,128)}) fusion(pred[1024,1792]{1,0:T(8,128)(4,1)S(1)} %fusion.2, bf16[1024,4,48]{0,2,1:T(8,128)(2,1)S(1)} %slice.216, bf16[1024,4,16]{0,2,1:T(8,128)(2,1)S(1)} %get-tuple-element.57, bf16[1024,4,64]{0,2,1:T(8,128)(2,1)S(1)} %bitcast.122, bf16[1024,4,48]{0,2,1:T(8,128)(2,1)S(1)} %slice.217, ...), kind=kOutput, calls=%fused_computation.5 | convolution fusion | flops 966717440 | bytes 32784384 | tf_op jit(solution)/shard_map/qhd,khd->hqk/dot_general | solution.py:60
  156.4 13.8 %exponential_reduce_fusion = f32[4,1024]{1,0:T(4,128)S(1)} fusion(f32[4,1024,1792]{2,1,0:T(8,128)} %get-tuple-element.66, f32[4,1024]{1,0:T(4,128)S(1)} %get-tuple-element.65, pred[1024,1792]{1,0:T(8,128)(4,1)S(1)} %fusion.2), kind=kLoop, calls=%fused_computation.3 | loop fusion | flops 29356032 | bytes 31227904 | tf_op jit(solution)/shard_map/reduce_sum | solution.py:160
  170.2 13.4 %all_gather.42 = bf16[1024,256]{0,1:T(8,128)(2,1)S(1)} all-gather(bf16[256,256]{0,1:T(8,128)(2,1)S(1)} %bitcast.131), channel_id=1, replica_groups=mesh['fsdp'=2,'ctx'=4,'tp'=4] {'ctx'}, dimensions={0}, use_global_device_ids=true | all-gather | bytes 655360 | tf_op jit(solution)/shard_map/all_gather | solution.py:148
  183.6 22.0 %multiply_reduce_fusion = (f32[4,1024]{1,0:T(4,128)S(1)}, f32[4,1024,1792]{2,1,0:T(8,128)}) fusion(f32[4,1024,1792]{2,1,0:T(8,128)} %get-tuple-element.66, f32[4,1024]{1,0:T(4,128)S(1)} %log_add_fusion, pred[1024,1792]{1,0:T(8,128)(4,1)S(1)} %fusion.2, bf16[1024,4,64]{0,2,1:T(8,128)(2,1)S(1)} %bitcast.128, bf16[768,4,64]{0,2,1:T(8,128)(2,1)S(1)} %slice_bitcast_fusion.4, ...), kind=kOutput, calls=%fused_computation.1 | convolution fusion | flops 978055168 | bytes 62029824 | tf_op jit(solution)/shard_map/qhd,khd->hqk/dot_general | solution.py:198
  205.6 24.6 %multiply_convert_fusion = bf16[4,1024,1792]{2,1,0:T(8,128)(2,1)} fusion(f32[4,1024,1792]{2,1,0:T(8,128)} %get-tuple-element.69, f32[4,1024,1792]{2,1,0:T(8,128)} %get-tuple-element.66, f32[4,1024]{1,0:T(4,128)S(1)} %get-tuple-element.68, f32[4,1024]{1,0:T(4,128)S(1)} %log_add_fusion, pred[1024,1792]{1,0:T(8,128)(4,1)S(1)} %fusion.2), kind=kLoop, calls=%fused_computation | loop fusion | flops 44040192 | bytes 75268096 | tf_op jit(solution)/shard_map/convert_element_type | solution.py:202
  230.2 7.8 fusion.30
  240.1 12.7 %convolution_bitcast_fusion = f32[1792,4,64]{0,2,1:T(8,128)S(1)} fusion(bf16[1024,4,64]{0,2,1:T(8,128)(2,1)S(1)} %bitcast.129, f32[4,1024,1792]{2,1,0:T(8,128)} %get-tuple-element.66, f32[4,1024]{1,0:T(4,128)S(1)} %log_add_fusion, pred[1024,1792]{1,0:T(8,128)(4,1)S(1)} %fusion.2), kind=kOutput, calls=%fused_computation.58 | convolution fusion | flops 968884224 | bytes 33570816 | tf_op jit(solution)/shard_map/hqk,qhd->khd/dot_general | solution.py:210
  254.7 9.7 fusion.35
  266.3 14.3 %convolution_convert_fusion.1 = bf16[4,64,1024]{2,1,0:T(8,128)(2,1)} fusion(bf16[768,4,64]{0,2,1:T(8,128)(2,1)} %copy-done.13, bf16[1024,4,64]{0,2,1:T(8,128)(2,1)} %bitcast.116, f32[4,1024,1792]{2,1,0:T(8,128)} %get-tuple-element.66, f32[4,1024]{1,0:T(4,128)S(1)} %log_add_fusion, pred[1024,1792]{1,0:T(8,128)(4,1)S(1)} %fusion.2), kind=kOutput, calls=%fused_computation.75 | convolution fusion | flops 970981376 | bytes 32653312 | tf_op jit(solution)/shard_map/hqk,khd->qhd/dot_general | solution.py:162
  280.9 3.9 fusion.42
  284.8 16.0 %multiply_convert_fusion.1 = (bf16[1024,1024]{1,0:T(8,128)(2,1)}, f32[1024,1024]{1,0:T(8,128)}, f32[1024,1024]{1,0:T(8,128)}) fusion(f32[1024]{0:T(1024)S(1)} %copy-done.28, bf16[1024,1024]{1,0:T(8,128)(2,1)} %all-gather.12.cloned.1.call-done, f32[1024]{0:T(1024)S(1)} %bitcast.147, f32[1024]{0:T(1024)S(1)} %bitcast.138, f32[1024]{0:T(1024)S(1)} %fusion.57, ...), kind=kOutput, calls=%fused_computation.41 | convolution fusion | flops 2226126848 | bytes 14700544 | tf_op jit(solution)/shard_map/dot_general | solution.py:165
  300.9 9.1 convert_reduce_fusion.2
  311.3 4.4 fusion.81
  319.6 5.6 reduce-scatter.9.cloned.1.call-done
  328.9 3.8 fusion.82
  333.0 6.0 convolution_convert_fusion
  339.1 3.3 fusion.76
  342.5 5.3 fusion.31
  347.9 6.2 fusion.67
  354.1 6.4 fusion.75
  361.1 13.6 %all-gather.4 = bf16[8,1,128]{2,1,0:T(2,128)(2,1)S(1)} all-gather(bf16[1,1,128]{2,1,0:T(2,128)(2,1)S(1)} %bitcast.154), channel_id=1, replica_groups=mesh['fsdp'=2,'ctx'=4,'tp'=4] {'fsdp','ctx'}, dimensions={0}, use_global_device_ids=true | all-gather | bytes 2304 | tf_op jit(solution)/shard_map/all_gather | solution.py:94
  374.8 13.4 %all-gather.5 = bf16[8,1,128]{2,1,0:T(2,128)(2,1)S(1)} all-gather(bf16[1,1,128]{2,1,0:T(2,128)(2,1)S(1)} %bitcast.155), channel_id=1, replica_groups=mesh['fsdp'=2,'ctx'=4,'tp'=4] {'fsdp','ctx'}, dimensions={0}, use_global_device_ids=true | all-gather | bytes 2304 | tf_op jit(solution)/shard_map/all_gather | solution.py:95
  389.5 370.9 %all-reduce.16.cloned.1.call-done = (f32[1024,1024]{1,0:T(8,128)}, f32[1024,1024]{1,0:T(8,128)}, f32[1024,1024]{1,0:T(8,128)}) async-done(((f32[1024,1024]{1,0:T(8,128)}, f32[1024,1024]{1,0:T(8,128)}, f32[1024,1024]{1,0:T(8,128)}), (f32[1024,1024]{1,0:T(8,128)}, f32[1024,1024]{1,0:T(8,128)}, f32[1024,1024]{1,0:T(8,128)})) %all-reduce.16.cloned.1.call-update) | async-done | bytes 12582928 | tf_op jit(solution)/shard_map/psum | solution.py:170
  760.4 4.7 fusion.79
  765.1 83.7 %all-reduce.14.cloned.1.call-done = bf16[1024,1024]{1,0:T(8,128)(2,1)} async-done(((bf16[1024,1024]{1,0:T(8,128)(2,1)}), bf16[1024,1024]{1,0:T(8,128)(2,1)}) %all-reduce.14.cloned.1.call-update) | async-done | bytes 2097168 | tf_op jit(solution)/shard_map/psum | solution.py:171
  848.8 9.3 fusion.18
  858.1 5.4 convert_reduce_fusion.1
  863.5 26.6 %all-reduce.9 = (f32[3,256]{1,0:T(4,128)}, f32[1024]{0:T(1024)S(1)}, f32[1024]{0:T(1024)}, f32[1024]{0:T(1024)S(1)}, f32[1024]{0:T(1024)S(1)}, /*index=5*/f32[1024]{0:T(1024)S(1)}, f32[1024]{0:T(1024)S(1)}) all-reduce(f32[3,256]{1,0:T(4,128)S(1)} %reshape.336, ...), channel_id=1, replica_groups=mesh['fsdp'=2,'ctx'=4,'tp'=4] {'fsdp','ctx'}, use_global_device_ids=true, to_apply=%region_17.18 | all-reduce | flops 6912 | bytes 55296 | tf_op jit(solution)/shard_map/psum | solution.py:266
  892.5 4.0 slice.168
  896.4 1.9 slice.152
  898.3 2.3 slice_bitcast_fusion
  901.7 36.9 %reduce-scatter.11.cloned.1.call-done = f32[128,3,256]{2,0,1:T(8,128)} async-done(((f32[1024,3,256]{2,0,1:T(8,128)}), f32[128,3,256]{2,0,1:T(8,128)}) %reduce-scatter.11.cloned.1.call-update) | async-done | bytes 393232 | tf_op jit(solution)/shard_map/reduce_scatter | solution.py:256
  938.6 55.1 %reduce-scatter.15.cloned.1.call-done = f32[128,1024]{1,0:T(8,128)} async-done(((f32[1024,1024]{1,0:T(8,128)}), f32[128,1024]{1,0:T(8,128)}) %reduce-scatter.15.cloned.1.call-update) | async-done | bytes 524304 | tf_op jit(solution)/shard_map/reduce_scatter | solution.py:258
  993.8 55.6 %reduce-scatter.17.cloned.1.call-done = f32[1024,128]{1,0:T(8,128)} async-done(((f32[1024,1024]{1,0:T(8,128)}), f32[1024,128]{1,0:T(8,128)}) %reduce-scatter.17.cloned.1.call-update) | async-done | bytes 524304 | tf_op jit(solution)/shard_map/reduce_scatter | solution.py:259
  (184 shorter events, 41.9 us)
Async XLA Ops:
  7.2 33.5 %copy-start.4 = (bf16[1,256,1024]{2,1,0:T(8,128)(2,1)S(1)}, bf16[1,256,1024]{2,1,0:T(8,128)(2,1)}, u32[]{:S(2)}) copy-start(bf16[1,256,1024]{2,1,0:T(8,128)(2,1)} %param.17) | copy-start | bytes 1572868
  7.2 33.5 %copy-start = (bf16[1,3,256,1024]{3,2,1,0:T(8,128)(2,1)S(1)}, bf16[1,3,256,1024]{3,2,1,0:T(8,128)(2,1)}, u32[]{:S(2)}) copy-start(bf16[1,3,256,1024]{3,2,1,0:T(8,128)(2,1)} %param.18) | copy-start | bytes 4718596
  7.2 34.3 %copy-start.32 = (s32[1,3]{1,0:T(1,128)S(1)}, s32[1,3]{1,0:T(1,128)}, u32[]{:S(2)}) copy-start(s32[1,3]{1,0:T(1,128)} %param.19) | copy-start | bytes 40
  7.2 34.6 %copy-start.10 = (bf16[1,256,1024]{2,1,0:T(8,128)(2,1)S(1)}, bf16[1,256,1024]{2,1,0:T(8,128)(2,1)}, u32[]{:S(2)}) copy-start(bf16[1,256,1024]{2,1,0:T(8,128)(2,1)} %param.32) | copy-start | bytes 1572868
  7.2 118.5 %all-gather.10.cloned.1.call-start = ((), (), s32[]{:S(2)}) async-start(), calls=%async_computation.6 | async-start | bytes 1769472 | tf_op jit(solution)/shard_map/all_gather | solution.py:90
  9.2 275.6 %all-gather.12.cloned.1.call-start = ((), (), s32[]{:S(2)}) async-start(), calls=%async_computation.7 | async-start | bytes 2359296 | tf_op jit(solution)/shard_map/all_gather | solution.py:92
  9.9 290.9 %all-gather.14.cloned.1.call-start = ((), (), s32[]{:S(2)}) async-start(), calls=%async_computation.8 | async-start | bytes 2359296 | tf_op jit(solution)/shard_map/all_gather | solution.py:93
  10.0 38.6 %collective-permute-start = (bf16[256,128]{1,0:T(8,128)(2,1)}, bf16[256,128]{1,0:T(8,128)(2,1)S(1)}, u32[]{:S(2)}, u32[]{:S(2)}) collective-permute-start(bf16[256,128]{1,0:T(8,128)(2,1)} %param.22), channel_id=1, source_target_pairs={{0,28},{4,0},{8,4},{12,8},{16,12},{20,16},{24,20},{28,24},{1,29},{... | collective-permute-start | bytes 196616 | tf_op jit(solution)/shard_map/ppermute | solution.py:16
  13.4 302.3 %reduce-scatter.7.cloned.1.call-start = ((), (), s32[]{:S(2)}) async-start(), calls=%async_computation.10 | async-start | bytes 1310720 | tf_op jit(solution)/shard_map/reduce_scatter | solution.py:214
  41.4 16.2 %copy-start.25 = (f32[1024]{0:T(1024)}, f32[1024]{0:T(1024)S(1)}, u32[]{:S(2)}) copy-start(f32[1024]{0:T(1024)S(1)} %fusion.19) | copy-start | bytes 12292
  41.4 7.1 copy-start.12
  48.6 7.6 collective-permute-start.1
  57.6 61.9 %collective-permute-start.2 = (bf16[256,512]{1,0:T(8,128)(2,1)}, bf16[256,512]{1,0:T(8,128)(2,1)}, u32[]{:S(2)}, u32[]{:S(2)}) collective-permute-start(bf16[256,512]{1,0:T(8,128)(2,1)} %pad_maximum_fusion.8), channel_id=1, source_target_pairs={{0,16},{4,20},{8,24},{12,28},{16,0},{20,4},{24,8},{28,12},{1,17},{... | collective-permute-start | bytes 786440 | tf_op jit(solution)/shard_map/ppermute | solution.py:16
  72.0 57.3 %copy-start.23 = (f32[8,1,128]{2,1,0:T(1,128)}, f32[8,1,128]{2,1,0:T(1,128)S(1)}, u32[]{:S(2)}) copy-start(f32[8,1,128]{2,1,0:T(1,128)S(1)} %convert_element_type.144) | copy-start | bytes 12292
  130.0 53.5 %copy-start.13 = (bf16[768,4,64]{0,2,1:T(8,128)(2,1)}, bf16[768,4,64]{0,2,1:T(8,128)(2,1)S(1)}, u32[]{:S(2)}) copy-start(bf16[768,4,64]{0,2,1:T(8,128)(2,1)S(1)} %slice_bitcast_fusion.4) | copy-start | bytes 1179652
  156.3 27.2 %copy-start.20 = (bf16[1024,256]{0,1:T(8,128)(2,1)S(1)}, bf16[1024,256]{0,1:T(8,128)(2,1)}, u32[]{:S(2)}) copy-start(bf16[1024,256]{0,1:T(8,128)(2,1)} %convolution_convert_fusion.2) | copy-start | bytes 1572868
  183.6 22.0 %copy-start.9 = (bf16[1024,256]{0,1:T(8,128)(2,1)}, bf16[1024,256]{0,1:T(8,128)(2,1)S(1)}, u32[]{:S(2)}) copy-start(bf16[1024,256]{0,1:T(8,128)(2,1)S(1)} %all_gather.42) | copy-start | bytes 1572868
  266.3 58.9 %reduce-scatter.9.cloned.1.call-start = ((), (), s32[]{:S(2)}) async-start(), calls=%async_computation.11 | async-start | bytes 1310720 | tf_op jit(solution)/shard_map/reduce_scatter | solution.py:220
  280.7 4.2 copy-start.5
  280.7 4.2 copy-start.28
  280.7 4.2 copy-start.30
  280.7 479.7 %all-reduce.16.cloned.1.call-start = ((), (), s32[]{:S(2)}) async-start(), calls=%async_computation.16 | async-start | bytes 25165824 | tf_op jit(solution)/shard_map/psum | solution.py:170
  284.8 16.0 %copy-start.11 = (bf16[1,256,1024]{2,1,0:T(8,128)(2,1)S(1)}, bf16[1,256,1024]{2,1,0:T(8,128)(2,1)}, u32[]{:S(2)}) copy-start(bf16[1,256,1024]{2,1,0:T(8,128)(2,1)} %param.32) | copy-start | bytes 1572868
  300.9 10.4 copy-start.35
  310.0 1.3 copy-start.39
  311.3 4.4 copy-start.6
  311.3 5.2 copy-start.19
  311.3 5.3 copy-start.21
  315.7 3.8 copy-start.14
  325.2 3.7 copy-start.36
  332.7 516.0 %all-reduce.14.cloned.1.call-start = ((), (), s32[]{:S(2)}) async-start(), calls=%async_computation.9 | async-start | bytes 4194304 | tf_op jit(solution)/shard_map/psum | solution.py:171
  333.0 6.1 copy-start.16
  339.0 3.4 copy-start.24
  339.0 3.5 copy-start.29
  339.0 562.7 %reduce-scatter.13.cloned.1.call-start = ((), (), s32[]{:S(2)}) async-start(), calls=%async_computation.13 | async-start | bytes 1179648 | tf_op jit(solution)/shard_map/reduce_scatter | solution.py:257
  342.4 596.2 %reduce-scatter.11.cloned.1.call-start = ((), (), s32[]{:S(2)}) async-start(), calls=%async_computation.12 | async-start | bytes 3538944 | tf_op jit(solution)/shard_map/reduce_scatter | solution.py:256
  342.5 5.4 copy-start.31
  347.8 646.0 %reduce-scatter.15.cloned.1.call-start = ((), (), s32[]{:S(2)}) async-start(), calls=%async_computation.14 | async-start | bytes 4718592 | tf_op jit(solution)/shard_map/reduce_scatter | solution.py:258
  354.1 695.4 %reduce-scatter.17.cloned.1.call-start = ((), (), s32[]{:S(2)}) async-start(), calls=%async_computation.15 | async-start | bytes 4718592 | tf_op jit(solution)/shard_map/reduce_scatter | solution.py:259
  360.5 14.3 %copy-start.34 = (bf16[128]{0:T(256)(128)(2,1)S(1)}, bf16[128]{0:T(256)(128)(2,1)}, u32[]{:S(2)}) copy-start(bf16[128]{0:T(256)(128)(2,1)} %param.27) | copy-start | bytes 772
  360.5 27.7 %copy-start.37 = (u32[32]{0:T(128)S(1)}, u32[32]{0:T(128)}, u32[]{:S(2)}) copy-start(u32[32]{0:T(128)} %constant.152) | copy-start | bytes 388
  760.4 4.7 copy-start.26
  848.8 9.3 copy-start.1
  848.8 9.3 copy-start.2
  848.8 9.3 copy-start.7
  858.1 5.4 copy-start.27
  890.1 6.4 copy-start.3
  890.1 159.3 %copy-start.38 = (f32[128]{0:T(128)}, f32[128]{0:T(128)S(1)}, u32[]{:S(2)}) copy-start(f32[128]{0:T(128)S(1)} %dynamic-slice.1) | copy-start | bytes 1540
  (6 other events, 5.3 us)
Sparse Core Ops, SparseCore 0:
  10.5 32.4 all-gather.9
  44.9 28.5 all-gather.11
  75.3 28.2 all-gather.13
  266.4 27.4 reduce-scatter.6
  297.4 27.7 reduce-scatter.8
  332.9 427.4 all-reduce.15
  763.3 85.4 all-reduce.13
  852.8 35.1 reduce-scatter.12
  892.4 46.2 reduce-scatter.10
  942.4 51.3 reduce-scatter.14
  998.1 51.2 reduce-scatter.16
